TPU v7x, 512 devices: a whole 4x8x8 slice. The times are simulated.
512 devices in a mesh: site: 16 (over z, core), col: 32 (over x, y).
Axes of the slice: x: 4, y: 8, z: 8, core: 2. Of those that a mesh axis runs over, the one named last changes fastest.
Arguments:
- state_prev: float32 [128, 128, 8192], P('site', None, 'col'), may hold values from -6 to 6
- state_cur: float32 [128, 128, 8192], P('site', None, 'col'), may hold values from -6 to 6
- occupancy: int32 [4, 128, 128], replicated, may hold values 0 or 1
- panel_order: int32 [32], replicated, may hold values from 0 to 31, each once
Outputs:
- ortho_states: float32 [128, 128, 8192], P('site', None, 'col')
- growth: float32 [2, 256], replicated
Inputs may be any that keep to these rules, and one draw needn't show every extreme that they name: panel_order holds each panel number once.
All inputs are finite; a program needn't handle non-finite values.
Results may differ from a plain program's by a relative error of at most 0.000075.
Values sent between devices are 32-bit elements; how exact they have to be, the bound alone decides.
No kernel may reach another device: no remote copies, remote signals or barrier semaphores. Data moves between devices by JAX's collectives and lax.ppermute only.
A program may use at most 64 MiB of HBM per device.

v0:
```python
import jax
import jax.numpy as jnp
from jax import lax
from jax.sharding import PartitionSpec as P

STEPS = 4
PANEL = 256


ENERGY = 0.5
RESCALE = 0.015625


def from_root(value, axis, root):
    mine = lax.axis_index(axis) == root
    return lax.psum(jnp.where(mine, value, jnp.zeros_like(value)), axis)


def padded_2(value, sides, width):
    for axis, dim in sides:
        size, length = (lax.axis_size(axis), value.shape[dim])
        up = [(i, (i + 1) % size) for i in range(size)]
        down = [(j, i) for i, j in up]
        last = lax.slice_in_dim(value, length - width, length, axis=dim)
        leading = lax.slice_in_dim(value, 0, width, axis=dim)
        before = lax.ppermute(last, axis, up)
        after = lax.ppermute(leading, axis, down)
        value = jnp.concatenate([before, value, after], axis=dim)
    return value


def product(left, right):
    return jnp.dot(left, right, precision=lax.Precision.HIGHEST, preferred_element_type=jnp.float32)


def fetch_panel(flat, panel):
    count = PANEL // flat.shape[1]
    pieces = from_root(flat, "col", panel * count + 0)
    return pieces


def apply_inverse(lower, block):
    return jax.scipy.linalg.solve_triangular(lower, block.T, lower=True).T


def sweep_panel(flat, panel):
    block = fetch_panel(flat, panel)
    lower = jnp.linalg.cholesky(lax.psum(product(block.T, block), "site"))
    ortho = apply_inverse(lower, block)
    flat = flat - product(ortho, lax.psum(product(ortho.T, flat), "site"))
    return (flat, lower, ortho)


def place(result, ortho, panel, side):
    width = result.shape[1]
    offset = (lax.axis_index("col") - panel * (PANEL // width)) * width
    inside = jnp.logical_and(offset >= 0, offset < PANEL)
    return jnp.where(inside, ortho * float(side), result)


def on_device(state_prev, state_cur, occupancy, panel_order):
    rows, side, width = state_cur.shape
    start = lax.axis_index("site") * rows
    local_mask = lax.dynamic_slice_in_dim(occupancy, start, rows, 1)
    previous, current = (state_prev, state_cur)
    for turn in range(STEPS):
        weights = local_mask[turn].astype(jnp.float32)[:, :, None]
        padded = padded_2(current, (("site", 0),), 1)
        neighbours = padded[2:] + padded[:-2] + jnp.roll(current, 1, 1) + jnp.roll(current, -1, 1)
        previous, current = (current, weights * (ENERGY * current - neighbours - previous))
    flat = current.reshape(rows * side, width)
    first_panel = panel_order[0]
    second_panel = panel_order[1]
    flat, first_lower, first_q = sweep_panel(flat, first_panel)
    flat, second_lower, second_q = sweep_panel(flat, second_panel)
    result = flat * RESCALE
    result = place(result, first_q, first_panel, side)
    result = place(result, second_q, second_panel, side)
    growth = jnp.stack([jnp.log(jnp.diagonal(first_lower)), jnp.log(jnp.diagonal(second_lower))])
    return (result.reshape(rows, side, width), growth)


def solution(mesh):
    return jax.shard_map(
        on_device,
        mesh=mesh,
        in_specs=(P("site", None, "col"), P("site", None, "col"), P(), P()),
        out_specs=(P("site", None, "col"), P()),
        check_vma=False,
    )
```

profile of v0, /device:TPU:1, one launch (start us, length us, event | category | flops | bytes accessed | tf_op | source)
XLA Modules:
  0.0 974.7 jit_solution(11955733928134964861)
XLA Ops:
  8.2 6.9 collective-permute-start
  16.0 2.8 fusion.74
  20.8 1.9 fusion.26
  22.9 3.1 collective-permute-start.2
  27.3 2.5 collective-permute-done.3
  30.5 4.8 collective-permute-start.4
  37.8 3.7 collective-permute-start.6
  46.1 155.3 %all-reduce.8.cloned.1.call-done = f32[1024,256]{0,1:T(8,128)} async-done(((f32[1024,256]{0,1:T(8,128)}), f32[1024,256]{0,1:T(8,128)}) %all-reduce.8.cloned.1.call-update) | async-done | bytes 1048592 | tf_op jit(solution)/shard_map/psum | solution.py:16
  201.3 3.3 fusion.78
  205.2 116.5 %all-reduce.10.cloned.1.call-done = f32[256,256]{0,1:T(8,128)} async-done(((f32[256,256]{0,1:T(8,128)}), f32[256,256]{0,1:T(8,128)}) %all-reduce.10.cloned.1.call-update) | async-done | bytes 262160 | tf_op jit(solution)/shard_map/psum | solution.py:48
  323.0 11.7 %cholesky.130 = f32[128,128]{1,0:T(8,128)S(1)} custom-call(f32[128,128]{1,0:T(8,128)S(1)} %cholesky.194), custom_call_target="Cholesky" | custom-call | tf_op jit(solution)/shard_map/jit(cholesky)/cholesky | solution.py:48
  334.7 9.8 %custom-call.17 = f32[1,128,128]{1,2,0:T(8,128)S(1)} custom-call(f32[1,128,128]{2,1,0:T(8,128)S(1)} %get-tuple-element.83), custom_call_target="InvertDiagBlocksLowerTriangular" | custom-call | tf_op jit(solution)/shard_map/jit(cholesky)/cholesky | solution.py:48
  345.0 11.7 %cholesky.147 = f32[128,128]{1,0:T(8,128)S(1)} custom-call(f32[128,128]{1,0:T(8,128)S(1)} %convolution_subtract_fusion.5), custom_call_target="Cholesky" | custom-call | tf_op jit(solution)/shard_map/jit(cholesky)/cholesky | solution.py:48
  358.9 4.2 while.4
  363.1 19.7 %custom-call.18 = f32[2,128,128]{1,2,0:T(8,128)S(1)} custom-call(f32[2,128,128]{2,1,0:T(8,128)S(1)} %get-tuple-element.18), custom_call_target="InvertDiagBlocksLowerTriangular" | custom-call | tf_op jit(solution)/shard_map/jit(_solve_triangular)/triangular_solve | solution.py:43
  384.7 1.7 fusion.28
  387.2 113.8 %all-reduce.12.cloned.1.call-done = f32[256,256]{1,0:T(8,128)} async-done(((f32[256,256]{1,0:T(8,128)}), f32[256,256]{1,0:T(8,128)}) %all-reduce.12.cloned.1.call-update) | async-done | bytes 262160 | tf_op jit(solution)/shard_map/psum | solution.py:50
  500.9 3.4 broadcast_select_fusion
  504.4 156.2 %all-reduce.14.cloned.1.call-done = f32[1024,256]{0,1:T(8,128)} async-done(((f32[1024,256]{0,1:T(8,128)}), f32[1024,256]{0,1:T(8,128)}) %all-reduce.14.cloned.1.call-update) | async-done | bytes 1048592 | tf_op jit(solution)/shard_map/psum | solution.py:16
  660.6 3.3 fusion.79
  664.1 116.9 %all-reduce.16.cloned.1.call-done = f32[256,256]{0,1:T(8,128)} async-done(((f32[256,256]{0,1:T(8,128)}), f32[256,256]{0,1:T(8,128)}) %all-reduce.16.cloned.1.call-update) | async-done | bytes 262160 | tf_op jit(solution)/shard_map/psum | solution.py:48
  782.2 11.7 %cholesky.164 = f32[128,128]{1,0:T(8,128)S(1)} custom-call(f32[128,128]{1,0:T(8,128)S(1)} %cholesky.197), custom_call_target="Cholesky" | custom-call | tf_op jit(solution)/shard_map/jit(cholesky)/cholesky | solution.py:48
  794.6 9.8 %custom-call.19 = f32[1,128,128]{1,2,0:T(8,128)S(1)} custom-call(f32[1,128,128]{2,1,0:T(8,128)S(1)} %get-tuple-element.79), custom_call_target="InvertDiagBlocksLowerTriangular" | custom-call | tf_op jit(solution)/shard_map/jit(cholesky)/cholesky | solution.py:48
  804.9 11.7 %cholesky.181 = f32[128,128]{1,0:T(8,128)S(1)} custom-call(f32[128,128]{1,0:T(8,128)S(1)} %convolution_subtract_fusion.4), custom_call_target="Cholesky" | custom-call | tf_op jit(solution)/shard_map/jit(cholesky)/cholesky | solution.py:48
  819.5 4.1 while.5
  823.6 19.7 %custom-call.20 = f32[2,128,128]{1,2,0:T(8,128)S(1)} custom-call(f32[2,128,128]{2,1,0:T(8,128)S(1)} %get-tuple-element.19), custom_call_target="InvertDiagBlocksLowerTriangular" | custom-call | tf_op jit(solution)/shard_map/jit(_solve_triangular)/triangular_solve | solution.py:43
  845.2 1.7 fusion.27
  848.2 2.3 gather_fusion
  850.6 2.3 gather_fusion.1
  853.5 107.9 %all-reduce.18.cloned.1.call-done = f32[256,256]{1,0:T(8,128)} async-done(((f32[256,256]{1,0:T(8,128)}), f32[256,256]{1,0:T(8,128)}) %all-reduce.18.cloned.1.call-update) | async-done | bytes 262160 | tf_op jit(solution)/shard_map/psum | solution.py:50
  961.4 3.6 fusion.2
  965.0 2.5 copy.27
  (112 shorter events, 32.0 us)
Async XLA Ops:
  7.2 194.2 %all-reduce.8.cloned.1.call-start = ((), (), s32[]{:S(2)}) async-start(), calls=%async_computation | async-start | bytes 2097152 | tf_op jit(solution)/shard_map/psum | solution.py:16
  8.2 12.5 %collective-permute-start = (f32[1,128,256]{2,1,0:T(8,128)S(1)}, f32[1,128,256]{2,1,0:T(8,128)S(1)}, u32[]{:S(2)}, u32[]{:S(2)}) collective-permute-start(f32[1,128,256]{2,1,0:T(8,128)S(1)} %get-tuple-element.70), channel_id=1, source_target_pairs={{32,0},{64,32},{96,64},{128,96},{160,128},{192,160},{224,192},{256... | collective-permute-start | bytes 393224 | tf_op jit(solution)/shard_map/ppermute | solution.py:27
  15.1 5.7 collective-permute-start.1
  16.0 2.8 copy-start.11
  16.0 4.8 copy-start
  22.9 4.4 collective-permute-start.2
  26.0 3.8 collective-permute-start.3
  30.5 5.8 collective-permute-start.4
  35.3 2.0 collective-permute-start.5
  37.8 5.1 collective-permute-start.6
  41.5 2.0 collective-permute-start.7
  43.9 1.0 copy-start.5
  46.0 275.7 %all-reduce.10.cloned.1.call-start = ((), (), s32[]{:S(2)}) async-start(), calls=%async_computation.1 | async-start | bytes 524288 | tf_op jit(solution)/shard_map/psum | solution.py:48
  204.6 296.3 %all-reduce.12.cloned.1.call-start = ((), (), s32[]{:S(2)}) async-start(), calls=%async_computation.2 | async-start | bytes 524288 | tf_op jit(solution)/shard_map/psum | solution.py:50
  321.7 1.2 copy-start.9
  344.8 38.0 %copy-start.1 = (f32[1024,256]{0,1:T(8,128)S(1)}, f32[1024,256]{0,1:T(8,128)}, u32[]{:S(2)}) copy-start(f32[1024,256]{0,1:T(8,128)} %all-reduce.8.cloned.1.call-done) | copy-start | bytes 3145732
  383.5 1.2 copy-start.6
  386.5 274.1 %all-reduce.14.cloned.1.call-start = ((), (), s32[]{:S(2)}) async-start(), calls=%async_computation.3 | async-start | bytes 2097152 | tf_op jit(solution)/shard_map/psum | solution.py:16
  504.3 276.6 %all-reduce.16.cloned.1.call-start = ((), (), s32[]{:S(2)}) async-start(), calls=%async_computation.4 | async-start | bytes 524288 | tf_op jit(solution)/shard_map/psum | solution.py:48
  663.9 297.6 %all-reduce.18.cloned.1.call-start = ((), (), s32[]{:S(2)}) async-start(), calls=%async_computation.5 | async-start | bytes 524288 | tf_op jit(solution)/shard_map/psum | solution.py:50
  781.0 1.2 copy-start.10
  804.6 38.6 %copy-start.2 = (f32[1024,256]{0,1:T(8,128)S(1)}, f32[1024,256]{0,1:T(8,128)}, u32[]{:S(2)}) copy-start(f32[1024,256]{0,1:T(8,128)} %all-reduce.14.cloned.1.call-done) | copy-start | bytes 3145732
  843.9 1.3 copy-start.3
  845.2 1.8 copy-start.7
  848.2 2.4 copy-start.8
  848.2 113.2 %copy-start.4 = (f32[1024,256]{0,1:T(8,128)S(1)}, f32[1024,256]{0,1:T(8,128)}, u32[]{:S(2)}) copy-start(f32[1024,256]{0,1:T(8,128)} %get-tuple-element.89) | copy-start | bytes 3145732
Sparse Core Ops, SparseCore 0:
  46.1 155.1 all-reduce.7
  204.7 116.9 all-reduce.9
  386.6 114.2 all-reduce.11
  504.8 155.7 all-reduce.13
  664.0 116.9 all-reduce.15
  847.1 114.3 all-reduce.17
where the time goes:
time: 979 us; the launch traced here: 975 us
  waiting for transfers between devices  774 us (79%)
  other arithmetic  115 us (12%)
  local copies, waits for them, and re-layouts  24.4 us (2%)
  matrix products  21.6 us (2%)
  between operations  19.9 us (2%)
  starting transfers between devices  19.5 us (2%)
    psum x2, waiting for transfers between devices, from_root(): return lax.psum(jnp.where(mine, value, jnp.zeros_like(value)), axis)  311 us
    psum x2, waiting for transfers between devices, sweep_panel(): lower = jnp.linalg.cholesky(lax.psum(product(block.T, block), 'site'))  233 us
    psum x2, waiting for transfers between devices, sweep_panel(): flat = flat - product(ortho, lax.psum(product(ortho.T, flat), 'site'))  222 us
    another operation x13, other arithmetic, sweep_panel(): lower = jnp.linalg.cholesky(lax.psum(product(block.T, block), 'site'))  68.7 us
    another operation x5, other arithmetic, apply_inverse(): return jax.scipy.linalg.solve_triangular(lower, block.T, lower=True).T  40.1 us
  transfers between devices with their start and end apart: 14, of which 12 were waited for; matrix products, arithmetic and copies ran while one was open for 1% of the time, Pallas kernels for 0%

commit v1 on v0

v1 whole, which is shorter than its diff:
```python
import jax
import jax.numpy as jnp
from jax import lax
from jax.sharding import PartitionSpec as P

STEPS = 4
PANEL = 256
ENERGY = 0.5
RESCALE = 0.015625

Z, CORE, X, Y = 8, 2, 4, 8


def x_shift(value, k):
    return lax.ppermute(value, "col", [(x * Y + y, ((x + k) % X) * Y + y) for x in range(X) for y in range(Y)])


def y_shift(value, k):
    return lax.ppermute(value, "col", [(x * Y + y, x * Y + (y + k) % Y) for x in range(X) for y in range(Y)])


def z_shift(value, k):
    return lax.ppermute(value, "site", [(z * CORE + c, ((z + k) % Z) * CORE + c) for z in range(Z) for c in range(CORE)])


def core_swap(value):
    return lax.ppermute(value, "site", [(z * CORE + c, z * CORE + 1 - c) for z in range(Z) for c in range(CORE)])


def padded_2(value):
    size, length = lax.axis_size("site"), value.shape[0]
    up = [(i, (i + 1) % size) for i in range(size)]
    down = [(j, i) for i, j in up]
    before = lax.ppermute(value[length - 1 :], "site", up)
    after = lax.ppermute(value[:1], "site", down)
    return jnp.concatenate([before, value, after], axis=0)


def product(left, right):
    return jnp.dot(left, right, precision=lax.Precision.HIGHEST, preferred_element_type=jnp.float32)


def product_t(left, right):
    dims = (((0,), (0,)), ((), ()))
    return lax.dot_general(left, right, dims, precision=lax.Precision.HIGHEST, preferred_element_type=jnp.float32)


def scatter(value, shift, me, size):
    rows = value.shape[0] // size
    out = []
    for k in range(size):
        piece = lax.dynamic_slice_in_dim(value, lax.rem(me + k, size) * rows, rows, 0)
        out.append(piece if k == 0 else shift(piece, k))
    return out


def gather(value, shift, me, size):
    parts = [value if k == 0 else shift(value, k) for k in range(size)]
    parts = parts[::-1]
    double = jnp.concatenate(parts + parts[:-1], axis=0)
    rows = value.shape[0]
    return lax.dynamic_slice_in_dim(double, (size - 1 - me) * rows, rows * size, 0)


def pick(parts, index):
    out = parts[0]
    for k in range(1, len(parts)):
        out = jnp.where(index == k, parts[k], out)
    return out


def fetch_panels(flat, panels):
    col = lax.axis_index("col")
    x, y = col // Y, lax.rem(col, Y)
    quarters = scatter(flat, x_shift, x, X)
    chosen = [pick(quarters, lax.rem(x - panel // Y + X, X)) for panel in panels]
    rows = chosen[0].shape[0] // Y
    both = jnp.concatenate([c.reshape(Y, rows, PANEL) for c in chosen], axis=1).reshape(-1, PANEL)
    eighths = scatter(both, y_shift, y, Y)
    mine = [
        pick([e[n * rows : (n + 1) * rows] for e in eighths], lax.rem(y - lax.rem(panel, Y) + Y, Y))
        for n, panel in enumerate(panels)
    ]
    both = gather(jnp.concatenate(mine, axis=0), y_shift, y, Y)
    both = gather(both, x_shift, x, X)
    both = both.reshape(X * Y, len(panels), rows, PANEL)
    return [both[:, n].reshape(-1, PANEL) for n in range(len(panels))]


def sum_sites(value):
    site = lax.axis_index("site")
    z, core = site // CORE, lax.rem(site, CORE)
    half = value.shape[0] // CORE
    keep = lax.dynamic_slice_in_dim(value, core * half, half, 0)
    give = lax.dynamic_slice_in_dim(value, (1 - core) * half, half, 0)
    value = keep + core_swap(give)
    parts = scatter(value, z_shift, z, Z)
    total = parts[0]
    for part in parts[1:]:
        total = total + part
    value = gather(total, z_shift, z, Z)
    other = core_swap(value)
    return jnp.where(core == 0, jnp.concatenate([value, other]), jnp.concatenate([other, value]))


def inverse_factor(gram):
    lower = jnp.linalg.cholesky(gram)
    inverse = jax.scipy.linalg.solve_triangular(lower, jnp.eye(PANEL, dtype=jnp.float32), lower=True)
    return inverse, jnp.log(jnp.diagonal(lower))


def on_device(state_prev, state_cur, occupancy, panel_order):
    rows, side, width = state_cur.shape
    start = lax.axis_index("site") * rows
    local_mask = lax.dynamic_slice_in_dim(occupancy, start, rows, 1)
    previous, current = (state_prev, state_cur)
    for turn in range(STEPS):
        weights = local_mask[turn].astype(jnp.float32)[:, :, None]
        padded = padded_2(current)
        neighbours = padded[2:] + padded[:-2] + jnp.roll(current, 1, 1) + jnp.roll(current, -1, 1)
        previous, current = (current, weights * (ENERGY * current - neighbours - previous))
    flat = current.reshape(rows * side, width)
    first, second = panel_order[0], panel_order[1]
    a, b = fetch_panels(flat, (first, second))

    ax, bx = product_t(a, flat), product_t(b, flat)
    aa, ab, bb = product_t(a, a), product_t(a, b), product_t(b, b)
    total = sum_sites(jnp.concatenate([aa, ab, bb, ax, bx], axis=0))
    aa, ab, bb, ax, bx = [total[n * PANEL : (n + 1) * PANEL] for n in range(5)]

    inverse_1, growth_1 = inverse_factor(aa)
    cross = product(inverse_1, ab)
    inverse_2, growth_2 = inverse_factor(bb - product_t(cross, cross))
    inner_1 = product(inverse_1, ax)
    inner_2 = product(inverse_2, bx - product_t(cross, inner_1))

    col = lax.axis_index("col")
    is_first, is_second = col == first, col == second
    eye = jnp.eye(PANEL, dtype=jnp.float32) * (-float(side))
    zero = jnp.zeros_like(eye)
    inner_1 = jnp.where(is_first, eye, jnp.where(is_second, zero, inner_1 * RESCALE))
    inner_2 = jnp.where(is_first, zero, jnp.where(is_second, eye, inner_2 * RESCALE))
    weight_b = product_t(inverse_2, inner_2)
    weight_a = product_t(inverse_1, inner_1 - product(cross, weight_b))
    scale = jnp.where(jnp.logical_or(is_first, is_second), 0.0, RESCALE)
    both = jnp.concatenate([a, b], axis=1)
    weight = jnp.concatenate([weight_a, weight_b], axis=0)
    result = flat * scale - product(both, weight)
    return (result.reshape(rows, side, width), jnp.stack([growth_1, growth_2]))


def solution(mesh):
    return jax.shard_map(
        on_device,
        mesh=mesh,
        in_specs=(P("site", None, "col"), P("site", None, "col"), P(), P()),
        out_specs=(P("site", None, "col"), P()),
        check_vma=False,
    )
```

time: 979 us -> 449 us (0.46)
  waiting for transfers between devices: 774 us -> 64.1 us
  starting transfers between devices: 19.5 us -> 154 us
  local copies, waits for them, and re-layouts: 24.4 us -> 44.4 us
  other arithmetic: 115 us -> 133 us
  matrix products: 21.6 us -> 35.6 us
    psum x6 -> x0, waiting for transfers between devices: 766 us -> none  [the longest x2 311 us: from_root(): return lax.psum(jnp.where(mine, value, jnp.zeros_like(value)), axis)]
    ppermute x8 -> x44, starting transfers between devices: 18.5 us -> 154 us  [the longest x14 53.3 us: z_shift(): lax.ppermute(value, 'site', [(z * CORE + c, (z + k) % Z * CORE + c) for z...]
    ppermute x8 -> x44, waiting for transfers between devices: 7.64 us -> 64.1 us  [the longest x14 28.7 us: z_shift(): lax.ppermute(value, 'site', [(z * CORE + c, (z + k) % Z * CORE + c) for z...]
    dot_general x0 -> x9, matrix products: none -> 14.3 us  [product_t(): lax.dot_general(left, right, dims, precision=lax.Precision.HIGHEST, prefe...]
    another operation x19, other arithmetic: 109 us -> 122 us  [the longest x13 76.6 us: inverse_factor(): lower = jnp.linalg.cholesky(gram)]
  transfers between devices with their start and end apart: 14 -> 44, of which waited for: 12 -> 21; matrix products, arithmetic and copies ran while one was open for 1% -> 1% of each run, Pallas kernels for 0% -> 0%
where the time goes in v1:
time: 449 us; the launch traced here: 442 us
  starting transfers between devices  154 us (34%)
  other arithmetic  133 us (30%)
  waiting for transfers between devices  64.1 us (14%)
  local copies, waits for them, and re-layouts  44.4 us (10%)
  matrix products  35.6 us (8%)
  between operations  11.1 us (2%)
    another operation x13, other arithmetic, inverse_factor(): lower = jnp.linalg.cholesky(gram)  76.6 us
    ppermute x14, starting transfers between devices, z_shift(): lax.ppermute(value, 'site', [(z * CORE + c, (z + k) % Z * CORE + c) for z...  53.3 us
    ppermute x14, starting transfers between devices, y_shift(): lax.ppermute(value, 'col', [(x * Y + y, x * Y + (y + k) % Y) for x in ran...  52.8 us
    another operation x5, other arithmetic, inverse_factor(): jax.scipy.linalg.solve_triangular(lower, jnp.eye(PANEL, dtype=jnp.float32...  45.1 us
    ppermute x14, waiting for transfers between devices, z_shift(): lax.ppermute(value, 'site', [(z * CORE + c, (z + k) % Z * CORE + c) for z...  28.7 us
    ppermute x4, starting transfers between devices, padded_2(): after = lax.ppermute(value[:1], 'site', down)  19.2 us
    ppermute x6, waiting for transfers between devices, x_shift(): lax.ppermute(value, 'col', [(x * Y + y, (x + k) % X * Y + y) for x in ran...  19.2 us
    ppermute x6, starting transfers between devices, x_shift(): lax.ppermute(value, 'col', [(x * Y + y, (x + k) % X * Y + y) for x in ran...  18.8 us
  transfers between devices with their start and end apart: 44, of which 21 were waited for; matrix products, arithmetic and copies ran while one was open for 1% of the time, Pallas kernels for 0%

profile of v1, /device:TPU:1, one launch (start us, length us, event | category | flops | bytes accessed | tf_op | source)
XLA Modules:
  0.0 442.3 jit_solution(3823874373995316779)
XLA Ops:
  2.3 6.9 %collective-permute-start = (f32[1,128,256]{2,1,0:T(8,128)}, f32[1,128,256]{2,1,0:T(8,128)S(1)}, u32[]{:S(2)}, u32[]{:S(2)}) collective-permute-start(f32[1,128,256]{2,1,0:T(8,128)} %get-tuple-element.73), channel_id=1, source_target_pairs={{32,0},{64,32},{96,64},{128,96},{160,128},{192,160},{224,192},{256... | collective-permute-start | bytes 393224 | tf_op jit(solution)/shard_map/ppermute | solution.py:35
  14.9 4.8 %collective-permute-start.2 = (f32[1,128,256]{2,1,0:T(8,128)S(1)}, f32[1,128,256]{2,1,0:T(8,128)S(1)}, u32[]{:S(2)}, u32[]{:S(2)}) collective-permute-start(f32[1,128,256]{2,1,0:T(8,128)S(1)} %get-tuple-element.67), channel_id=1, source_target_pairs={{32,0},{64,32},{96,64},{128,96},{160,128},{192,160},{224,192},{256... | collective-permute-start | bytes 393224 | tf_op jit(solution)/shard_map/ppermute | solution.py:35
  22.3 3.9 collective-permute-start.4
  51.3 5.1 %collective-permute-start.11 = (f32[64,256]{1,0:T(8,128)S(1)}, f32[64,256]{1,0:T(8,128)S(1)}, u32[]{:S(2)}, u32[]{:S(2)}) collective-permute-start(f32[64,256]{1,0:T(8,128)S(1)} %get-tuple-element.82), channel_id=1, source_target_pairs={{0,7},{1,0},{2,1},{3,2},{4,3},{5,4},{6,5},{7,6},{8,15},{9,8},{10,9... | collective-permute-start | bytes 196616 | tf_op jit(solution)/shard_map/ppermute | solution.py:19
  63.0 5.7 %collective-permute-start.14 = (f32[64,256]{1,0:T(8,128)S(1)}, f32[64,256]{1,0:T(8,128)S(1)}, u32[]{:S(2)}, u32[]{:S(2)}) collective-permute-start(f32[64,256]{1,0:T(8,128)S(1)} %get-tuple-element.86), channel_id=1, source_target_pairs={{0,4},{1,5},{2,6},{3,7},{4,0},{5,1},{6,2},{7,3},{8,12},{9,13},{10,... | collective-permute-start | bytes 196616 | tf_op jit(solution)/shard_map/ppermute | solution.py:19
  70.6 4.8 %collective-permute-start.16 = (f32[64,256]{1,0:T(8,128)S(1)}, f32[64,256]{1,0:T(8,128)S(1)}, u32[]{:S(2)}, u32[]{:S(2)}) collective-permute-start(f32[64,256]{1,0:T(8,128)S(1)} %get-tuple-element.84), channel_id=1, source_target_pairs={{0,2},{1,3},{2,4},{3,5},{4,6},{5,7},{6,0},{7,1},{8,10},{9,11},{10,... | collective-permute-start | bytes 196616 | tf_op jit(solution)/shard_map/ppermute | solution.py:19
  87.7 5.4 %collective-permute-start.20 = (f32[64,256]{1,0:T(8,128)S(1)}, f32[64,256]{1,0:T(8,128)S(1)}, u32[]{:S(2)}, u32[]{:S(2)}) collective-permute-start(f32[64,256]{1,0:T(8,128)S(1)} %pad_maximum_fusion.16), channel_id=1, source_target_pairs={{0,5},{1,6},{2,7},{3,0},{4,1},{5,2},{6,3},{7,4},{8,13},{9,14},{10,... | collective-permute-start | bytes 196616 | tf_op jit(solution)/shard_map/ppermute | solution.py:19
  100.5 4.4 collective-permute-start.23
  111.4 4.3 collective-permute-start.25
  120.3 6.9 %collective-permute-done.25 = f32[512,256]{1,0:T(8,128)S(1)} collective-permute-done((f32[512,256]{1,0:T(8,128)S(1)}, f32[512,256]{1,0:T(8,128)S(1)}, u32[]{:S(2)}, u32[]{:S(2)}) %collective-permute-start.25) | collective-permute-done | bytes 524320 | tf_op jit(solution)/shard_map/ppermute | solution.py:15
  127.2 11.6 %collective-permute-done.27 = f32[512,256]{1,0:T(8,128)S(1)} collective-permute-done((f32[512,256]{1,0:T(8,128)S(1)}, f32[512,256]{1,0:T(8,128)S(1)}, u32[]{:S(2)}, u32[]{:S(2)}) %collective-permute-start.27) | collective-permute-done | bytes 524320 | tf_op jit(solution)/shard_map/ppermute | solution.py:15
  150.7 7.6 %collective-permute-start.28 = (f32[640,256]{0,1:T(8,128)}, f32[640,256]{0,1:T(8,128)}, u32[]{:S(2)}, u32[]{:S(2)}) collective-permute-start(f32[640,256]{0,1:T(8,128)} %constant_dynamic-slice_fusion.13), channel_id=1, source_target_pairs={{0,32},{32,0},{64,96},{96,64},{128,160},{160,128},{192,224},{224,1... | collective-permute-start | bytes 1966088 | tf_op jit(solution)/shard_map/ppermute | solution.py:27
  165.5 6.3 %collective-permute-start.30 = (f32[80,256]{0,1:T(8,128)S(1)}, f32[80,256]{0,1:T(8,128)S(1)}, u32[]{:S(2)}, u32[]{:S(2)}) collective-permute-start(f32[80,256]{0,1:T(8,128)S(1)} %get-tuple-element.81), channel_id=1, source_target_pairs={{0,128},{32,160},{64,192},{96,224},{128,256},{160,288},{192,320},{... | collective-permute-start | bytes 245768 | tf_op jit(solution)/shard_map/ppermute | solution.py:23
  174.3 5.1 %collective-permute-start.32 = (f32[80,256]{0,1:T(8,128)}, f32[80,256]{0,1:T(8,128)}, u32[]{:S(2)}, u32[]{:S(2)}) collective-permute-start(f32[80,256]{0,1:T(8,128)} %get-tuple-element.79), channel_id=1, source_target_pairs={{0,256},{32,288},{64,320},{96,352},{128,384},{160,416},{192,448},{... | collective-permute-start | bytes 245768 | tf_op jit(solution)/shard_map/ppermute | solution.py:23
  179.4 6.4 %collective-permute-start.33 = (f32[80,256]{0,1:T(8,128)}, f32[80,256]{0,1:T(8,128)}, u32[]{:S(2)}, u32[]{:S(2)}) collective-permute-start(f32[80,256]{0,1:T(8,128)} %get-tuple-element.78), channel_id=1, source_target_pairs={{0,320},{32,352},{64,384},{96,416},{128,448},{160,480},{192,0},{22... | collective-permute-start | bytes 245768 | tf_op jit(solution)/shard_map/ppermute | solution.py:23
  191.1 3.8 collective-permute-done.32
  194.9 7.9 %collective-permute-done.34 = f32[80,256]{0,1:T(8,128)} collective-permute-done((f32[80,256]{0,1:T(8,128)S(1)}, f32[80,256]{0,1:T(8,128)}, u32[]{:S(2)}, u32[]{:S(2)}) %collective-permute-start.34) | collective-permute-done | bytes 81952 | tf_op jit(solution)/shard_map/ppermute | solution.py:23
  206.4 4.0 collective-permute-start.36
  213.4 4.7 %collective-permute-start.38 = (f32[80,256]{0,1:T(8,128)S(1)}, f32[80,256]{0,1:T(8,128)}, u32[]{:S(2)}, u32[]{:S(2)}) collective-permute-start(f32[80,256]{0,1:T(8,128)S(1)} %add_add_fusion), channel_id=1, source_target_pairs={{0,320},{32,352},{64,384},{96,416},{128,448},{160,480},{192,0},{22... | collective-permute-start | bytes 245768 | tf_op jit(solution)/shard_map/ppermute | solution.py:23
  225.2 5.5 %collective-permute-start.41 = (f32[80,256]{0,1:T(8,128)S(1)}, f32[80,256]{0,1:T(8,128)}, u32[]{:S(2)}, u32[]{:S(2)}) collective-permute-start(f32[80,256]{0,1:T(8,128)S(1)} %add_add_fusion), channel_id=1, source_target_pairs={{0,128},{32,160},{64,192},{96,224},{128,256},{160,288},{192,320},{... | collective-permute-start | bytes 245768 | tf_op jit(solution)/shard_map/ppermute | solution.py:23
  233.0 7.0 %collective-permute-done.40 = f32[80,256]{0,1:T(8,128)} collective-permute-done((f32[80,256]{0,1:T(8,128)S(1)}, f32[80,256]{0,1:T(8,128)}, u32[]{:S(2)}, u32[]{:S(2)}) %collective-permute-start.40) | collective-permute-done | bytes 81952 | tf_op jit(solution)/shard_map/ppermute | solution.py:23
  240.0 7.8 %collective-permute-done.42 = f32[80,256]{0,1:T(8,128)} collective-permute-done((f32[80,256]{0,1:T(8,128)S(1)}, f32[80,256]{0,1:T(8,128)}, u32[]{:S(2)}, u32[]{:S(2)}) %collective-permute-start.42) | collective-permute-done | bytes 81952 | tf_op jit(solution)/shard_map/ppermute | solution.py:23
  264.4 11.7 %cholesky.130 = f32[128,128]{1,0:T(8,128)S(1)} custom-call(f32[128,128]{1,0:T(8,128)S(1)} %cholesky.194), custom_call_target="Cholesky" | custom-call | tf_op jit(solution)/shard_map/jit(cholesky)/cholesky | solution.py:107
  276.9 9.8 %custom-call.17 = f32[1,128,128]{1,2,0:T(8,128)S(1)} custom-call(f32[1,128,128]{2,1,0:T(8,128)S(1)} %get-tuple-element.100), custom_call_target="InvertDiagBlocksLowerTriangular" | custom-call | tf_op jit(solution)/shard_map/jit(cholesky)/cholesky | solution.py:107
  289.5 11.7 %cholesky.147 = f32[128,128]{1,0:T(8,128)S(1)} custom-call(f32[128,128]{1,0:T(8,128)S(1)} %convolution_subtract_fusion.4), custom_call_target="Cholesky" | custom-call | tf_op jit(solution)/shard_map/jit(cholesky)/cholesky | solution.py:107
  305.8 5.7 %while.4 = (s32[]{:T(128)}, f32[256,256]{1,0:T(8,128)}, s32[2,2]{1,0:T(2,128)S(1)}, f32[2,128,128]{2,1,0:T(8,128)S(1)}, s32[]{:T(128)}) while((s32[]{:T(128)}, f32[256,256]{1,0:T(8,128)}, s32[2,2]{1,0:T(2,128)S(1)}, f32[2,128,128]{2,1,0:T(8,128)S(1)}, s32[]{:T(128)}) %tuple.81), condition=%wide.while_cond, body=%wide.while_body.sunk | while | flops 2 | bytes 131181 | solution.py:108
  311.6 20.4 %custom-call.18 = f32[2,128,128]{1,2,0:T(8,128)} custom-call(f32[2,128,128]{2,1,0:T(8,128)S(1)} %get-tuple-element.18), custom_call_target="InvertDiagBlocksLowerTriangular" | custom-call | tf_op jit(solution)/shard_map/jit(_solve_triangular)/triangular_solve | solution.py:108
  345.4 13.2 %cholesky.164 = f32[128,128]{1,0:T(8,128)} custom-call(f32[128,128]{1,0:T(8,128)} %cholesky.197), custom_call_target="Cholesky" | custom-call | tf_op jit(solution)/shard_map/jit(cholesky)/cholesky | solution.py:107
  361.6 11.3 %custom-call.19 = f32[1,128,128]{1,2,0:T(8,128)} custom-call(f32[1,128,128]{2,1,0:T(8,128)} %get-tuple-element.96), custom_call_target="InvertDiagBlocksLowerTriangular" | custom-call | tf_op jit(solution)/shard_map/jit(cholesky)/cholesky | solution.py:107
  376.3 13.4 %cholesky.181 = f32[128,128]{1,0:T(8,128)} custom-call(f32[128,128]{1,0:T(8,128)} %convolution_subtract_fusion.3), custom_call_target="Cholesky" | custom-call | tf_op jit(solution)/shard_map/jit(cholesky)/cholesky | solution.py:107
  401.2 8.2 %while.5 = (s32[]{:T(128)}, f32[256,256]{1,0:T(8,128)}, s32[2,2]{1,0:T(2,128)}, f32[2,128,128]{2,1,0:T(8,128)}, s32[]{:T(128)}) while((s32[]{:T(128)}, f32[256,256]{1,0:T(8,128)}, s32[2,2]{1,0:T(2,128)}, f32[2,128,128]{2,1,0:T(8,128)}, s32[]{:T(128)}) %tuple.87), condition=%wide.while_cond.clone, body=%wide.while_body.clone.sunk | while | flops 2 | bytes 132705 | solution.py:108
  409.4 21.1 %custom-call.20 = f32[2,128,128]{1,2,0:T(8,128)} custom-call(f32[2,128,128]{2,1,0:T(8,128)} %get-tuple-element.19), custom_call_target="InvertDiagBlocksLowerTriangular" | custom-call | tf_op jit(solution)/shard_map/jit(_solve_triangular)/triangular_solve | solution.py:108
  (219 shorter events, 188.8 us)
Async XLA Ops:
  2.3 9.6 %collective-permute-start = (f32[1,128,256]{2,1,0:T(8,128)}, f32[1,128,256]{2,1,0:T(8,128)S(1)}, u32[]{:S(2)}, u32[]{:S(2)}) collective-permute-start(f32[1,128,256]{2,1,0:T(8,128)} %get-tuple-element.73), channel_id=1, source_target_pairs={{32,0},{64,32},{96,64},{128,96},{160,128},{192,160},{224,192},{256... | collective-permute-start | bytes 393224 | tf_op jit(solution)/shard_map/ppermute | solution.py:35
  34.9 15.6 %collective-permute-start.10 = (f32[256,256]{1,0:T(8,128)S(1)}, f32[256,256]{1,0:T(8,128)S(1)}, u32[]{:S(2)}, u32[]{:S(2)}) collective-permute-start(f32[256,256]{1,0:T(8,128)S(1)} %get-tuple-element.48), channel_id=1, source_target_pairs={{0,8},{1,9},{2,10},{3,11},{4,12},{5,13},{6,14},{7,15},{8,16},{9,17... | collective-permute-start | bytes 786440 | tf_op jit(solution)/shard_map/ppermute | solution.py:15
  38.0 12.5 %collective-permute-start.8 = (f32[256,256]{1,0:T(8,128)S(1)}, f32[256,256]{1,0:T(8,128)S(1)}, u32[]{:S(2)}, u32[]{:S(2)}) collective-permute-start(f32[256,256]{1,0:T(8,128)S(1)} %get-tuple-element.50), channel_id=1, source_target_pairs={{0,24},{1,25},{2,26},{3,27},{4,28},{5,29},{6,30},{7,31},{8,0},{9,1... | collective-permute-start | bytes 786440 | tf_op jit(solution)/shard_map/ppermute | solution.py:15
  41.4 9.8 %collective-permute-start.9 = (f32[256,256]{1,0:T(8,128)S(1)}, f32[256,256]{1,0:T(8,128)S(1)}, u32[]{:S(2)}, u32[]{:S(2)}) collective-permute-start(f32[256,256]{1,0:T(8,128)S(1)} %get-tuple-element.49), channel_id=1, source_target_pairs={{0,16},{1,17},{2,18},{3,19},{4,20},{5,21},{6,22},{7,23},{8,24},{9,... | collective-permute-start | bytes 786440 | tf_op jit(solution)/shard_map/ppermute | solution.py:15
  51.3 19.2 %collective-permute-start.11 = (f32[64,256]{1,0:T(8,128)S(1)}, f32[64,256]{1,0:T(8,128)S(1)}, u32[]{:S(2)}, u32[]{:S(2)}) collective-permute-start(f32[64,256]{1,0:T(8,128)S(1)} %get-tuple-element.82), channel_id=1, source_target_pairs={{0,7},{1,0},{2,1},{3,2},{4,3},{5,4},{6,5},{7,6},{8,15},{9,8},{10,9... | collective-permute-start | bytes 196616 | tf_op jit(solution)/shard_map/ppermute | solution.py:19
  56.4 19.0 %collective-permute-start.12 = (f32[64,256]{1,0:T(8,128)S(1)}, f32[64,256]{1,0:T(8,128)S(1)}, u32[]{:S(2)}, u32[]{:S(2)}) collective-permute-start(f32[64,256]{1,0:T(8,128)S(1)} %get-tuple-element.88), channel_id=1, source_target_pairs={{0,6},{1,7},{2,0},{3,1},{4,2},{5,3},{6,4},{7,5},{8,14},{9,15},{10,... | collective-permute-start | bytes 196616 | tf_op jit(solution)/shard_map/ppermute | solution.py:19
  60.2 18.5 %collective-permute-start.13 = (f32[64,256]{1,0:T(8,128)S(1)}, f32[64,256]{1,0:T(8,128)S(1)}, u32[]{:S(2)}, u32[]{:S(2)}) collective-permute-start(f32[64,256]{1,0:T(8,128)S(1)} %get-tuple-element.87), channel_id=1, source_target_pairs={{0,5},{1,6},{2,7},{3,0},{4,1},{5,2},{6,3},{7,4},{8,13},{9,14},{10,... | collective-permute-start | bytes 196616 | tf_op jit(solution)/shard_map/ppermute | solution.py:19
  63.0 15.7 %collective-permute-start.14 = (f32[64,256]{1,0:T(8,128)S(1)}, f32[64,256]{1,0:T(8,128)S(1)}, u32[]{:S(2)}, u32[]{:S(2)}) collective-permute-start(f32[64,256]{1,0:T(8,128)S(1)} %get-tuple-element.86), channel_id=1, source_target_pairs={{0,4},{1,5},{2,6},{3,7},{4,0},{5,1},{6,2},{7,3},{8,12},{9,13},{10,... | collective-permute-start | bytes 196616 | tf_op jit(solution)/shard_map/ppermute | solution.py:19
  68.6 10.1 %collective-permute-start.15 = (f32[64,256]{1,0:T(8,128)S(1)}, f32[64,256]{1,0:T(8,128)S(1)}, u32[]{:S(2)}, u32[]{:S(2)}) collective-permute-start(f32[64,256]{1,0:T(8,128)S(1)} %get-tuple-element.85), channel_id=1, source_target_pairs={{0,3},{1,4},{2,5},{3,6},{4,7},{5,0},{6,1},{7,2},{8,11},{9,12},{10,... | collective-permute-start | bytes 196616 | tf_op jit(solution)/shard_map/ppermute | solution.py:19
  82.6 17.9 %collective-permute-start.18 = (f32[64,256]{1,0:T(8,128)S(1)}, f32[64,256]{1,0:T(8,128)S(1)}, u32[]{:S(2)}, u32[]{:S(2)}) collective-permute-start(f32[64,256]{1,0:T(8,128)S(1)} %pad_maximum_fusion.16), channel_id=1, source_target_pairs={{0,7},{1,0},{2,1},{3,2},{4,3},{5,4},{6,5},{7,6},{8,15},{9,8},{10,9... | collective-permute-start | bytes 196616 | tf_op jit(solution)/shard_map/ppermute | solution.py:19
  85.8 19.2 %collective-permute-start.19 = (f32[64,256]{1,0:T(8,128)S(1)}, f32[64,256]{1,0:T(8,128)S(1)}, u32[]{:S(2)}, u32[]{:S(2)}) collective-permute-start(f32[64,256]{1,0:T(8,128)S(1)} %pad_maximum_fusion.16), channel_id=1, source_target_pairs={{0,6},{1,7},{2,0},{3,1},{4,2},{5,3},{6,4},{7,5},{8,14},{9,15},{10,... | collective-permute-start | bytes 196616 | tf_op jit(solution)/shard_map/ppermute | solution.py:19
  87.7 20.6 %collective-permute-start.20 = (f32[64,256]{1,0:T(8,128)S(1)}, f32[64,256]{1,0:T(8,128)S(1)}, u32[]{:S(2)}, u32[]{:S(2)}) collective-permute-start(f32[64,256]{1,0:T(8,128)S(1)} %pad_maximum_fusion.16), channel_id=1, source_target_pairs={{0,5},{1,6},{2,7},{3,0},{4,1},{5,2},{6,3},{7,4},{8,13},{9,14},{10,... | collective-permute-start | bytes 196616 | tf_op jit(solution)/shard_map/ppermute | solution.py:19
  93.1 15.2 %collective-permute-start.21 = (f32[64,256]{1,0:T(8,128)S(1)}, f32[64,256]{1,0:T(8,128)S(1)}, u32[]{:S(2)}, u32[]{:S(2)}) collective-permute-start(f32[64,256]{1,0:T(8,128)S(1)} %pad_maximum_fusion.16), channel_id=1, source_target_pairs={{0,4},{1,5},{2,6},{3,7},{4,0},{5,1},{6,2},{7,3},{8,12},{9,13},{10,... | collective-permute-start | bytes 196616 | tf_op jit(solution)/shard_map/ppermute | solution.py:19
  96.9 11.5 %collective-permute-start.22 = (f32[64,256]{1,0:T(8,128)S(1)}, f32[64,256]{1,0:T(8,128)S(1)}, u32[]{:S(2)}, u32[]{:S(2)}) collective-permute-start(f32[64,256]{1,0:T(8,128)S(1)} %pad_maximum_fusion.16), channel_id=1, source_target_pairs={{0,3},{1,4},{2,5},{3,6},{4,7},{5,0},{6,1},{7,2},{8,11},{9,12},{10,... | collective-permute-start | bytes 196616 | tf_op jit(solution)/shard_map/ppermute | solution.py:19
  111.4 15.8 %collective-permute-start.25 = (f32[512,256]{1,0:T(8,128)S(1)}, f32[512,256]{1,0:T(8,128)S(1)}, u32[]{:S(2)}, u32[]{:S(2)}) collective-permute-start(f32[512,256]{1,0:T(8,128)S(1)} %constant_dynamic-slice_fusion.15), channel_id=1, source_target_pairs={{0,24},{1,25},{2,26},{3,27},{4,28},{5,29},{6,30},{7,31},{8,0},{9,1... | collective-permute-start | bytes 1572872 | tf_op jit(solution)/shard_map/ppermute | solution.py:15
  115.6 11.6 %collective-permute-start.26 = (f32[512,256]{1,0:T(8,128)S(1)}, f32[512,256]{1,0:T(8,128)S(1)}, u32[]{:S(2)}, u32[]{:S(2)}) collective-permute-start(f32[512,256]{1,0:T(8,128)S(1)} %constant_dynamic-slice_fusion.15), channel_id=1, source_target_pairs={{0,16},{1,17},{2,18},{3,19},{4,20},{5,21},{6,22},{7,23},{8,24},{9,... | collective-permute-start | bytes 1572872 | tf_op jit(solution)/shard_map/ppermute | solution.py:15
  117.6 21.3 %collective-permute-start.27 = (f32[512,256]{1,0:T(8,128)S(1)}, f32[512,256]{1,0:T(8,128)S(1)}, u32[]{:S(2)}, u32[]{:S(2)}) collective-permute-start(f32[512,256]{1,0:T(8,128)S(1)} %constant_dynamic-slice_fusion.15), channel_id=1, source_target_pairs={{0,8},{1,9},{2,10},{3,11},{4,12},{5,13},{6,14},{7,15},{8,16},{9,17... | collective-permute-start | bytes 1572872 | tf_op jit(solution)/shard_map/ppermute | solution.py:15
  150.7 9.7 %collective-permute-start.28 = (f32[640,256]{0,1:T(8,128)}, f32[640,256]{0,1:T(8,128)}, u32[]{:S(2)}, u32[]{:S(2)}) collective-permute-start(f32[640,256]{0,1:T(8,128)} %constant_dynamic-slice_fusion.13), channel_id=1, source_target_pairs={{0,32},{32,0},{64,96},{96,64},{128,160},{160,128},{192,224},{224,1... | collective-permute-start | bytes 1966088 | tf_op jit(solution)/shard_map/ppermute | solution.py:27
  163.6 22.2 %collective-permute-start.29 = (f32[80,256]{0,1:T(8,128)S(1)}, f32[80,256]{0,1:T(8,128)S(1)}, u32[]{:S(2)}, u32[]{:S(2)}) collective-permute-start(f32[80,256]{0,1:T(8,128)S(1)} %get-tuple-element.75), channel_id=1, source_target_pairs={{0,64},{32,96},{64,128},{96,160},{128,192},{160,224},{192,256},{22... | collective-permute-start | bytes 245768 | tf_op jit(solution)/shard_map/ppermute | solution.py:23
  165.5 22.2 %collective-permute-start.30 = (f32[80,256]{0,1:T(8,128)S(1)}, f32[80,256]{0,1:T(8,128)S(1)}, u32[]{:S(2)}, u32[]{:S(2)}) collective-permute-start(f32[80,256]{0,1:T(8,128)S(1)} %get-tuple-element.81), channel_id=1, source_target_pairs={{0,128},{32,160},{64,192},{96,224},{128,256},{160,288},{192,320},{... | collective-permute-start | bytes 245768 | tf_op jit(solution)/shard_map/ppermute | solution.py:23
  171.8 19.2 %collective-permute-start.31 = (f32[80,256]{0,1:T(8,128)}, f32[80,256]{0,1:T(8,128)}, u32[]{:S(2)}, u32[]{:S(2)}) collective-permute-start(f32[80,256]{0,1:T(8,128)} %get-tuple-element.80), channel_id=1, source_target_pairs={{0,192},{32,224},{64,256},{96,288},{128,320},{160,352},{192,384},{... | collective-permute-start | bytes 245768 | tf_op jit(solution)/shard_map/ppermute | solution.py:23
  174.3 20.6 %collective-permute-start.32 = (f32[80,256]{0,1:T(8,128)}, f32[80,256]{0,1:T(8,128)}, u32[]{:S(2)}, u32[]{:S(2)}) collective-permute-start(f32[80,256]{0,1:T(8,128)} %get-tuple-element.79), channel_id=1, source_target_pairs={{0,256},{32,288},{64,320},{96,352},{128,384},{160,416},{192,448},{... | collective-permute-start | bytes 245768 | tf_op jit(solution)/shard_map/ppermute | solution.py:23
  179.4 15.5 %collective-permute-start.33 = (f32[80,256]{0,1:T(8,128)}, f32[80,256]{0,1:T(8,128)}, u32[]{:S(2)}, u32[]{:S(2)}) collective-permute-start(f32[80,256]{0,1:T(8,128)} %get-tuple-element.78), channel_id=1, source_target_pairs={{0,320},{32,352},{64,384},{96,416},{128,448},{160,480},{192,0},{22... | collective-permute-start | bytes 245768 | tf_op jit(solution)/shard_map/ppermute | solution.py:23
  185.8 17.1 %collective-permute-start.34 = (f32[80,256]{0,1:T(8,128)S(1)}, f32[80,256]{0,1:T(8,128)}, u32[]{:S(2)}, u32[]{:S(2)}) collective-permute-start(f32[80,256]{0,1:T(8,128)S(1)} %get-tuple-element.77), channel_id=1, source_target_pairs={{0,384},{32,416},{64,448},{96,480},{128,0},{160,32},{192,64},{224,... | collective-permute-start | bytes 245768 | tf_op jit(solution)/shard_map/ppermute | solution.py:23
  188.4 16.6 %collective-permute-start.35 = (f32[80,256]{0,1:T(8,128)S(1)}, f32[80,256]{0,1:T(8,128)}, u32[]{:S(2)}, u32[]{:S(2)}) collective-permute-start(f32[80,256]{0,1:T(8,128)S(1)} %get-tuple-element.76), channel_id=1, source_target_pairs={{0,448},{32,480},{64,0},{96,32},{128,64},{160,96},{192,128},{224,1... | collective-permute-start | bytes 245768 | tf_op jit(solution)/shard_map/ppermute | solution.py:23
  206.4 18.8 %collective-permute-start.36 = (f32[80,256]{0,1:T(8,128)S(1)}, f32[80,256]{0,1:T(8,128)S(1)}, u32[]{:S(2)}, u32[]{:S(2)}) collective-permute-start(f32[80,256]{0,1:T(8,128)S(1)} %add_add_fusion), channel_id=1, source_target_pairs={{0,448},{32,480},{64,0},{96,32},{128,64},{160,96},{192,128},{224,1... | collective-permute-start | bytes 245768 | tf_op jit(solution)/shard_map/ppermute | solution.py:23
  210.4 20.3 %collective-permute-start.37 = (f32[80,256]{0,1:T(8,128)S(1)}, f32[80,256]{0,1:T(8,128)S(1)}, u32[]{:S(2)}, u32[]{:S(2)}) collective-permute-start(f32[80,256]{0,1:T(8,128)S(1)} %add_add_fusion), channel_id=1, source_target_pairs={{0,384},{32,416},{64,448},{96,480},{128,0},{160,32},{192,64},{224,... | collective-permute-start | bytes 245768 | tf_op jit(solution)/shard_map/ppermute | solution.py:23
  213.4 19.6 %collective-permute-start.38 = (f32[80,256]{0,1:T(8,128)S(1)}, f32[80,256]{0,1:T(8,128)}, u32[]{:S(2)}, u32[]{:S(2)}) collective-permute-start(f32[80,256]{0,1:T(8,128)S(1)} %add_add_fusion), channel_id=1, source_target_pairs={{0,320},{32,352},{64,384},{96,416},{128,448},{160,480},{192,0},{22... | collective-permute-start | bytes 245768 | tf_op jit(solution)/shard_map/ppermute | solution.py:23
  218.1 15.0 %collective-permute-start.39 = (f32[80,256]{0,1:T(8,128)S(1)}, f32[80,256]{0,1:T(8,128)}, u32[]{:S(2)}, u32[]{:S(2)}) collective-permute-start(f32[80,256]{0,1:T(8,128)S(1)} %add_add_fusion), channel_id=1, source_target_pairs={{0,256},{32,288},{64,320},{96,352},{128,384},{160,416},{192,448},{... | collective-permute-start | bytes 245768 | tf_op jit(solution)/shard_map/ppermute | solution.py:23
  221.5 18.5 %collective-permute-start.40 = (f32[80,256]{0,1:T(8,128)S(1)}, f32[80,256]{0,1:T(8,128)}, u32[]{:S(2)}, u32[]{:S(2)}) collective-permute-start(f32[80,256]{0,1:T(8,128)S(1)} %add_add_fusion), channel_id=1, source_target_pairs={{0,192},{32,224},{64,256},{96,288},{128,320},{160,352},{192,384},{... | collective-permute-start | bytes 245768 | tf_op jit(solution)/shard_map/ppermute | solution.py:23
  225.2 14.8 %collective-permute-start.41 = (f32[80,256]{0,1:T(8,128)S(1)}, f32[80,256]{0,1:T(8,128)}, u32[]{:S(2)}, u32[]{:S(2)}) collective-permute-start(f32[80,256]{0,1:T(8,128)S(1)} %add_add_fusion), channel_id=1, source_target_pairs={{0,128},{32,160},{64,192},{96,224},{128,256},{160,288},{192,320},{... | collective-permute-start | bytes 245768 | tf_op jit(solution)/shard_map/ppermute | solution.py:23
  230.7 17.1 %collective-permute-start.42 = (f32[80,256]{0,1:T(8,128)S(1)}, f32[80,256]{0,1:T(8,128)}, u32[]{:S(2)}, u32[]{:S(2)}) collective-permute-start(f32[80,256]{0,1:T(8,128)S(1)} %add_add_fusion), channel_id=1, source_target_pairs={{0,64},{32,96},{64,128},{96,160},{128,192},{160,224},{192,256},{22... | collective-permute-start | bytes 245768 | tf_op jit(solution)/shard_map/ppermute | solution.py:23
  (27 other events, 224.2 us)
